TPU v7x, 128 devices: a whole 4x4x4 slice. The times are simulated.
128 devices in a mesh: section: 2 (over core), dp: 16 (over y, x), mp: 4 (over z).
Axes of the slice: x: 4, y: 4, z: 4, core: 2. Of those that a mesh axis runs over, the one named last changes fastest.
Arguments:
- out_grad: bfloat16 [512, 8192], P('dp', 'mp'), may hold values from -6 to 6
- upper_w: bfloat16 [2, 14336, 8192], P('section', 'dp', 'mp'), may hold values from -0.0625 to 0.0625
- lower_w: bfloat16 [2, 8192, 14336], P('section', 'mp', 'dp'), may hold values from -0.046875 to 0.046875
- upper_in: bfloat16 [2, 512, 14336], P('section', None, 'mp'), may hold values from -6 to 6
- lower_in: bfloat16 [2, 512, 8192], P('section', None, 'dp'), may hold values from -6 to 6
- upper_deriv: bfloat16 [2, 512, 14336], P('section', 'mp', 'dp'), may hold values from 0.3984375 to 1.5
- lower_deriv: bfloat16 [2, 512, 8192], P('section', 'dp', 'mp'), may hold values from 0.3984375 to 1.5
- proj_upper_in: bfloat16 [2, 64, 14336], P('section', None, 'mp'), may hold values from -0.046875 to 0.046875
- proj_upper_out: bfloat16 [2, 64, 8192], P('section', None, 'mp'), may hold values from -0.0625 to 0.0625
- proj_lower_in: bfloat16 [2, 64, 8192], P('section', None, 'dp'), may hold values from -0.0625 to 0.0625
- proj_lower_out: bfloat16 [2, 64, 14336], P('section', None, 'dp'), may hold values from -0.046875 to 0.046875
- window_ids: int32 [512], replicated, may hold values from 0 to 255
- window_slot: int32 [256], replicated, may hold values from 0 to 255, each once
Outputs:
- section_grads: bfloat16 [2, 512, 8192], P('section', 'dp', 'mp')
- sketches: float32 [2, 2, 256, 4096], P('section', None, ('dp', 'mp'))
Inputs may be any that keep to these rules, and one draw needn't show every extreme that they name: Each window has exactly one row: window_slot is a permutation.
All inputs are finite; a program needn't handle non-finite values.
Results may differ from a plain program's by a relative error of at most 0.0075.
Values may be sent and summed in bfloat16 or wider, within the bound.
No kernel may reach another device: no remote copies, remote signals or barrier semaphores. Data moves between devices by JAX's collectives and lax.ppermute only.
A program may use at most 128 MiB of HBM per device.

v0:
```python
import jax
import jax.numpy as jnp
from jax import lax
from jax.sharding import PartitionSpec as P


def from_behind(block, axis, distance):
    devices = range(lax.axis_size(axis))
    route = [(i - distance, i) for i in devices if i - distance in devices]
    return lax.ppermute(block, axis, route)


def times_t(left, right):
    return lax.dot_general(
        left, right, (((1,), (1,)), ((), ())), preferred_element_type=jnp.float32
    )


def token_lower(dp_src, mp_src, block_id, inner, tokens_dev, rows_block, quota):
    return dp_src * tokens_dev + block_id * rows_block + mp_src * quota + inner


def token_upper(dp_src, mp_src, block_id, inner, tokens_dev, rows_block, quota, ratio):
    flat_row = dp_src * quota + inner
    return (
        (mp_src * ratio + flat_row // rows_block) * tokens_dev
        + block_id * rows_block
        + flat_row % rows_block
    )


def slots_of(token_rows, window_ids, window_slot):
    total_tokens = window_ids.shape[0]
    picked = token_rows[:, None] == jnp.arange(total_tokens, dtype=jnp.int32)[None, :]
    window_row = jnp.sum(jnp.where(picked, window_ids[None, :], 0), axis=1)
    window_count = window_slot.shape[0]
    matched = window_row[:, None] == jnp.arange(window_count, dtype=jnp.int32)[None, :]
    return jnp.sum(jnp.where(matched, window_slot[None, :], 0), axis=1)


def outer_rows(factors, rank_size):
    left = factors[:, :rank_size]
    right = factors[:, rank_size:]
    return (left[:, :, None] * right[:, None, :]).reshape(factors.shape[0], rank_size * rank_size)


def window_sums(targets, factors, window_count, rank_size):
    matched = (targets[:, None] == jnp.arange(window_count, dtype=jnp.int32)[None, :]).astype(
        jnp.float32
    )
    return lax.dot_general(
        matched,
        outer_rows(factors, rank_size),
        (((0,), (0,)), ((), ())),
        precision=lax.Precision.HIGHEST,
        preferred_element_type=jnp.float32,
    )


def body(
    out_grad,
    upper_w,
    lower_w,
    upper_in,
    lower_in,
    upper_deriv,
    lower_deriv,
    proj_upper_in,
    proj_upper_out,
    proj_lower_in,
    proj_lower_out,
    window_ids,
    window_slot,
):
    section_count = lax.axis_size("section")
    dp_count = lax.axis_size("dp")
    mp_count = lax.axis_size("mp")
    section_index = lax.axis_index("section")
    dp_index = lax.axis_index("dp")
    mp_index = lax.axis_index("mp")
    tokens_dev = out_grad.shape[0]
    width_mp = out_grad.shape[1]
    width_ff = upper_deriv.shape[2]
    width_hidden = upper_in.shape[2]
    width_low = lower_in.shape[2]
    rank_size = proj_upper_in.shape[1]
    ratio = dp_count // mp_count
    block_count = 4
    rows_block = tokens_dev // block_count
    quota = rows_block // mp_count
    weight_up = upper_w[0]
    weight_low = lower_w[0]
    acts_upper = upper_in[0].reshape(dp_count, tokens_dev, width_hidden)
    acts_lower = lower_in[0].reshape(dp_count, tokens_dev, width_low)
    deriv_up = upper_deriv[0].reshape(ratio, tokens_dev, width_ff)
    deriv_low = lower_deriv[0]
    pin_up = proj_upper_in[0]
    pout_up = proj_upper_out[0]
    pin_low = proj_lower_in[0]
    pout_low = proj_lower_out[0]

    def advance(turn, carry):
        received, grads, factors_low, factors_up = carry
        block_id = turn - (section_count - 1 - section_index)
        is_live = (block_id >= 0) & (block_id < block_count)
        block_safe = jnp.clip(block_id, 0, block_count - 1)
        first_row = block_safe * rows_block
        top_block = lax.dynamic_slice_in_dim(out_grad, first_row, rows_block, 0)
        grad_up = jnp.where(section_index == section_count - 1, top_block, received)
        gathered_up = lax.all_gather(grad_up, "dp", axis=0, tiled=True)
        inputs_up = lax.dynamic_slice_in_dim(acts_upper, first_row, rows_block, 1).reshape(
            dp_count * rows_block, width_hidden
        )
        grad_rows = gathered_up
        input_rows = inputs_up
        summed_up = lax.psum_scatter(
            jnp.concatenate(
                [
                    times_t(grad_rows, weight_up),
                    times_t(input_rows, pin_up),
                    times_t(grad_rows, pout_up),
                ],
                axis=1,
            ),
            "mp",
            scatter_dimension=0,
            tiled=True,
        )
        scale_up = lax.dynamic_slice_in_dim(deriv_up, first_row, rows_block, 1).reshape(
            ratio * rows_block, width_ff
        )
        grad_mid = (summed_up[:, :width_ff] * scale_up.astype(jnp.float32)).astype(jnp.bfloat16)
        owned_up = lax.dynamic_slice_in_dim(summed_up[:, width_ff:], dp_index * quota, quota, 0)
        gathered_low = lax.all_gather(grad_mid, "mp", axis=0, tiled=True)
        inputs_low = lax.dynamic_slice_in_dim(acts_lower, first_row, rows_block, 1).reshape(
            dp_count * rows_block, width_low
        )
        grad_rows = gathered_low
        input_rows = inputs_low
        summed_low = lax.psum_scatter(
            jnp.concatenate(
                [
                    times_t(grad_rows, weight_low),
                    times_t(input_rows, pin_low),
                    times_t(grad_rows, pout_low),
                ],
                axis=1,
            ),
            "dp",
            scatter_dimension=0,
            tiled=True,
        )
        scale_low = lax.dynamic_slice_in_dim(deriv_low, first_row, rows_block, 0)
        grad_out = (summed_low[:, :width_mp] * scale_low.astype(jnp.float32)).astype(jnp.bfloat16)
        owned_low = lax.dynamic_slice_in_dim(summed_low[:, width_mp:], mp_index * quota, quota, 0)
        previous = lax.dynamic_slice_in_dim(grads, first_row, rows_block, 0)
        grads = lax.dynamic_update_slice_in_dim(
            grads, jnp.where(is_live, grad_out, previous), first_row, 0
        )
        prev_low = lax.dynamic_slice_in_dim(factors_low, block_safe, 1, 0)
        factors_low = lax.dynamic_update_slice_in_dim(
            factors_low, jnp.where(is_live, owned_low[None], prev_low), block_safe, 0
        )
        prev_up = lax.dynamic_slice_in_dim(factors_up, block_safe, 1, 0)
        factors_up = lax.dynamic_update_slice_in_dim(
            factors_up, jnp.where(is_live, owned_up[None], prev_up), block_safe, 0
        )
        received = from_behind(grad_out, "section", -1)
        return (received, grads, factors_low, factors_up)

    start_carry = (
        jnp.zeros((rows_block, width_mp), jnp.bfloat16),
        jnp.zeros((tokens_dev, width_mp), jnp.bfloat16),
        jnp.zeros((block_count, quota, 2 * rank_size), jnp.float32),
        jnp.zeros((block_count, quota, 2 * rank_size), jnp.float32),
    )
    _, grads, factors_low, factors_up = lax.fori_loop(
        0, block_count + section_count - 1, advance, start_carry
    )
    flat_low = factors_low.reshape(block_count * quota, 2 * rank_size)
    flat_up = factors_up.reshape(block_count * quota, 2 * rank_size)
    window_count = window_slot.shape[0]
    block_grid = jnp.arange(block_count, dtype=jnp.int32)[:, None]
    inner_grid = jnp.arange(quota, dtype=jnp.int32)[None, :]
    tokens_low = token_lower(
        dp_index, mp_index, block_grid, inner_grid, tokens_dev, rows_block, quota
    ).reshape(-1)
    tokens_up = token_upper(
        dp_index, mp_index, block_grid, inner_grid, tokens_dev, rows_block, quota, ratio
    ).reshape(-1)
    low_part = window_sums(
        slots_of(tokens_low, window_ids, window_slot), flat_low, window_count, rank_size
    )
    up_part = window_sums(
        slots_of(tokens_up, window_ids, window_slot), flat_up, window_count, rank_size
    )
    sketch = lax.psum_scatter(
        jnp.stack([low_part, up_part]), ("dp", "mp"), scatter_dimension=1, tiled=True
    )
    return (grads[None], sketch[None])


def solution(mesh):
    placed = (
        P("dp", "mp"),
        P("section", "dp", "mp"),
        P("section", "mp", "dp"),
        P("section", None, "mp"),
        P("section", None, "dp"),
        P("section", "mp", "dp"),
        P("section", "dp", "mp"),
        P("section", None, "mp"),
        P("section", None, "mp"),
        P("section", None, "dp"),
        P("section", None, "dp"),
        P(),
        P(),
    )
    return jax.shard_map(
        body,
        mesh=mesh,
        in_specs=placed,
        out_specs=(P("section", "dp", "mp"), P("section", None, ("dp", "mp"), None)),
        check_vma=False,
    )
```

profile of v0, /device:TPU:0, one launch (start us, length us, event | category | flops | bytes accessed | tf_op | source)
XLA Modules:
  0.0 996.2 jit_solution(14661798061254032778)
XLA Ops:
  8.1 801.4 %while.21 = (s32[]{:T(128)}, bf16[8,2048]{1,0:T(8,128)(2,1)S(1)}, bf16[32,2048]{1,0:T(8,128)(2,1)S(1)}, f32[4,2,128]{2,1,0:T(2,128)S(1)}, f32[4,2,128]{2,1,0:T(2...) while((s32[]{:T(128)}, bf16[8,2048]{1,0:T(8,128)(2,1)S(1)}, ...), condition=%wide.region_3.4_spmd, body=%wide.region_0.3_spmd.sunk | while | flops 1055576576 | bytes 28484304 | solution.py:177
  9.0 24.3 %all_gather.20 = bf16[128,2048]{1,0:T(8,128)(2,1)S(1)} all-gather(bf16[8,2048]{1,0:T(8,128)(2,1)S(1)} %dynamic-slice_select_fusion.2), channel_id=1, replica_groups=mesh['section'=2,'dp'=16,'mp'=4] {'dp'}, dimensions={0}, use_global_device_ids=true | all-gather | bytes 557056 | tf_op jit(solution)/shard_map/while/body/eval_jaxpr/all_gather | solution.py:110
  41.6 20.9 %reduce-scatter.3.cloned.1.call-done = f32[32,1024]{1,0:T(8,128)} async-done(((f32[128,1024]{1,0:T(8,128)}), f32[32,1024]{1,0:T(8,128)}) %reduce-scatter.3.cloned.1.call-update) | async-done | bytes 131088 | tf_op jit(solution)/shard_map/while/body/eval_jaxpr/reduce_scatter | solution.py:116
  63.5 12.2 %all_gather.21 = bf16[128,896]{1,0:T(8,128)(2,1)S(1)} all-gather(bf16[32,896]{1,0:T(8,128)(2,1)S(1)} %fusion.69), channel_id=1, replica_groups=mesh['section'=2,'dp'=16,'mp'=4] {'mp'}, dimensions={0}, use_global_device_ids=true | all-gather | bytes 286720 | tf_op jit(solution)/shard_map/while/body/eval_jaxpr/all_gather | solution.py:134
  81.8 85.1 %all-reduce.9.cloned.1.call-done = f32[128,2176]{1,0:T(8,128)} async-done(((f32[128,2176]{1,0:T(8,128)}), f32[128,2176]{1,0:T(8,128)}) %all-reduce.9.cloned.1.call-update) | async-done | bytes 1114128 | tf_op jit(solution)/shard_map/while
  171.7 23.1 %all_gather.20 = bf16[128,2048]{1,0:T(8,128)(2,1)S(1)} all-gather(bf16[8,2048]{1,0:T(8,128)(2,1)S(1)} %dynamic-slice_select_fusion.2), channel_id=1, replica_groups=mesh['section'=2,'dp'=16,'mp'=4] {'dp'}, dimensions={0}, use_global_device_ids=true | all-gather | bytes 557056 | tf_op jit(solution)/shard_map/while/body/eval_jaxpr/all_gather | solution.py:110
  203.0 19.2 %reduce-scatter.3.cloned.1.call-done = f32[32,1024]{1,0:T(8,128)} async-done(((f32[128,1024]{1,0:T(8,128)}), f32[32,1024]{1,0:T(8,128)}) %reduce-scatter.3.cloned.1.call-update) | async-done | bytes 131088 | tf_op jit(solution)/shard_map/while/body/eval_jaxpr/reduce_scatter | solution.py:116
  223.1 12.2 %all_gather.21 = bf16[128,896]{1,0:T(8,128)(2,1)S(1)} all-gather(bf16[32,896]{1,0:T(8,128)(2,1)S(1)} %fusion.69), channel_id=1, replica_groups=mesh['section'=2,'dp'=16,'mp'=4] {'mp'}, dimensions={0}, use_global_device_ids=true | all-gather | bytes 286720 | tf_op jit(solution)/shard_map/while/body/eval_jaxpr/all_gather | solution.py:134
  241.4 85.1 %all-reduce.9.cloned.1.call-done = f32[128,2176]{1,0:T(8,128)} async-done(((f32[128,2176]{1,0:T(8,128)}), f32[128,2176]{1,0:T(8,128)}) %all-reduce.9.cloned.1.call-update) | async-done | bytes 1114128 | tf_op jit(solution)/shard_map/while
  331.3 23.1 %all_gather.20 = bf16[128,2048]{1,0:T(8,128)(2,1)S(1)} all-gather(bf16[8,2048]{1,0:T(8,128)(2,1)S(1)} %dynamic-slice_select_fusion.2), channel_id=1, replica_groups=mesh['section'=2,'dp'=16,'mp'=4] {'dp'}, dimensions={0}, use_global_device_ids=true | all-gather | bytes 557056 | tf_op jit(solution)/shard_map/while/body/eval_jaxpr/all_gather | solution.py:110
  362.7 19.2 %reduce-scatter.3.cloned.1.call-done = f32[32,1024]{1,0:T(8,128)} async-done(((f32[128,1024]{1,0:T(8,128)}), f32[32,1024]{1,0:T(8,128)}) %reduce-scatter.3.cloned.1.call-update) | async-done | bytes 131088 | tf_op jit(solution)/shard_map/while/body/eval_jaxpr/reduce_scatter | solution.py:116
  382.8 12.2 %all_gather.21 = bf16[128,896]{1,0:T(8,128)(2,1)S(1)} all-gather(bf16[32,896]{1,0:T(8,128)(2,1)S(1)} %fusion.69), channel_id=1, replica_groups=mesh['section'=2,'dp'=16,'mp'=4] {'mp'}, dimensions={0}, use_global_device_ids=true | all-gather | bytes 286720 | tf_op jit(solution)/shard_map/while/body/eval_jaxpr/all_gather | solution.py:134
  401.1 85.1 %all-reduce.9.cloned.1.call-done = f32[128,2176]{1,0:T(8,128)} async-done(((f32[128,2176]{1,0:T(8,128)}), f32[128,2176]{1,0:T(8,128)}) %all-reduce.9.cloned.1.call-update) | async-done | bytes 1114128 | tf_op jit(solution)/shard_map/while
  491.0 23.1 %all_gather.20 = bf16[128,2048]{1,0:T(8,128)(2,1)S(1)} all-gather(bf16[8,2048]{1,0:T(8,128)(2,1)S(1)} %dynamic-slice_select_fusion.2), channel_id=1, replica_groups=mesh['section'=2,'dp'=16,'mp'=4] {'dp'}, dimensions={0}, use_global_device_ids=true | all-gather | bytes 557056 | tf_op jit(solution)/shard_map/while/body/eval_jaxpr/all_gather | solution.py:110
  522.4 19.2 %reduce-scatter.3.cloned.1.call-done = f32[32,1024]{1,0:T(8,128)} async-done(((f32[128,1024]{1,0:T(8,128)}), f32[32,1024]{1,0:T(8,128)}) %reduce-scatter.3.cloned.1.call-update) | async-done | bytes 131088 | tf_op jit(solution)/shard_map/while/body/eval_jaxpr/reduce_scatter | solution.py:116
  542.5 12.2 %all_gather.21 = bf16[128,896]{1,0:T(8,128)(2,1)S(1)} all-gather(bf16[32,896]{1,0:T(8,128)(2,1)S(1)} %fusion.69), channel_id=1, replica_groups=mesh['section'=2,'dp'=16,'mp'=4] {'mp'}, dimensions={0}, use_global_device_ids=true | all-gather | bytes 286720 | tf_op jit(solution)/shard_map/while/body/eval_jaxpr/all_gather | solution.py:134
  560.8 85.1 %all-reduce.9.cloned.1.call-done = f32[128,2176]{1,0:T(8,128)} async-done(((f32[128,2176]{1,0:T(8,128)}), f32[128,2176]{1,0:T(8,128)}) %all-reduce.9.cloned.1.call-update) | async-done | bytes 1114128 | tf_op jit(solution)/shard_map/while
  650.7 23.1 %all_gather.20 = bf16[128,2048]{1,0:T(8,128)(2,1)S(1)} all-gather(bf16[8,2048]{1,0:T(8,128)(2,1)S(1)} %dynamic-slice_select_fusion.2), channel_id=1, replica_groups=mesh['section'=2,'dp'=16,'mp'=4] {'dp'}, dimensions={0}, use_global_device_ids=true | all-gather | bytes 557056 | tf_op jit(solution)/shard_map/while/body/eval_jaxpr/all_gather | solution.py:110
  675.1 3.4 fusion.68
  682.1 19.2 %reduce-scatter.3.cloned.1.call-done = f32[32,1024]{1,0:T(8,128)} async-done(((f32[128,1024]{1,0:T(8,128)}), f32[32,1024]{1,0:T(8,128)}) %reduce-scatter.3.cloned.1.call-update) | async-done | bytes 131088 | tf_op jit(solution)/shard_map/while/body/eval_jaxpr/reduce_scatter | solution.py:116
  702.1 12.2 %all_gather.21 = bf16[128,896]{1,0:T(8,128)(2,1)S(1)} all-gather(bf16[32,896]{1,0:T(8,128)(2,1)S(1)} %fusion.69), channel_id=1, replica_groups=mesh['section'=2,'dp'=16,'mp'=4] {'mp'}, dimensions={0}, use_global_device_ids=true | all-gather | bytes 286720 | tf_op jit(solution)/shard_map/while/body/eval_jaxpr/all_gather | solution.py:134
  720.5 85.1 %all-reduce.9.cloned.1.call-done = f32[128,2176]{1,0:T(8,128)} async-done(((f32[128,2176]{1,0:T(8,128)}), f32[128,2176]{1,0:T(8,128)}) %all-reduce.9.cloned.1.call-update) | async-done | bytes 1114128 | tf_op jit(solution)/shard_map/while
  814.8 3.8 pad_maximum_fusion.1
  820.5 166.7 %all-reduce.7.cloned.1.call-done = f32[2,256,4096]{2,1,0:T(8,128)} async-done(((f32[2,256,4096]{2,1,0:T(8,128)}), f32[2,256,4096]{2,1,0:T(8,128)}) %all-reduce.7.cloned.1.call-update) | async-done | bytes 8388624
  (187 shorter events, 101.5 us)
Async XLA Ops:
  8.1 802.5 %copy-start.4 = (s32[512]{0:T(512)S(1)}, s32[512]{0:T(512)}, u32[]{:S(2)}) copy-start(s32[512]{0:T(512)} %param.26) | copy-start | bytes 6148
  8.1 802.7 %copy-start.5 = (s32[256]{0:T(256)S(1)}, s32[256]{0:T(256)}, u32[]{:S(2)}) copy-start(s32[256]{0:T(256)} %param.27) | copy-start | bytes 3076
  8.1 29.9 %copy-start = (bf16[64,3584]{1,0:T(8,128)(2,1)S(1)}, bf16[64,3584]{1,0:T(8,128)(2,1)}, u32[]{:S(2)}) copy-start(bf16[64,3584]{1,0:T(8,128)(2,1)} %get-tuple-element.691) | copy-start | bytes 1376260 | tf_op jit(solution)/shard_map/while
  8.1 54.4 %reduce-scatter.3.cloned.1.call-start = ((), (), s32[]{:S(2)}) async-start(), calls=%async_computation.2 | async-start | bytes 655360 | tf_op jit(solution)/shard_map/while/body/eval_jaxpr/reduce_scatter | solution.py:116
  39.5 39.5 %copy-start.1 = (bf16[64,896]{1,0:T(8,128)(2,1)S(1)}, bf16[64,896]{1,0:T(8,128)(2,1)}, u32[]{:S(2)}) copy-start(bf16[64,896]{1,0:T(8,128)(2,1)} %get-tuple-element.697) | copy-start | bytes 344068 | tf_op jit(solution)/shard_map/while
  40.5 126.4 %all-reduce.9.cloned.1.call-start = ((), (), s32[]{:S(2)}) async-start(), calls=%async_computation.3 | async-start | bytes 2228224 | tf_op jit(solution)/shard_map/while
  167.7 3.1 collective-permute-start
  170.8 51.4 %reduce-scatter.3.cloned.1.call-start = ((), (), s32[]{:S(2)}) async-start(), calls=%async_computation.2 | async-start | bytes 655360 | tf_op jit(solution)/shard_map/while/body/eval_jaxpr/reduce_scatter | solution.py:116
  201.0 37.7 %copy-start.1 = (bf16[64,896]{1,0:T(8,128)(2,1)S(1)}, bf16[64,896]{1,0:T(8,128)(2,1)}, u32[]{:S(2)}) copy-start(bf16[64,896]{1,0:T(8,128)(2,1)} %get-tuple-element.697) | copy-start | bytes 344068 | tf_op jit(solution)/shard_map/while
  201.9 124.6 %all-reduce.9.cloned.1.call-start = ((), (), s32[]{:S(2)}) async-start(), calls=%async_computation.3 | async-start | bytes 2228224 | tf_op jit(solution)/shard_map/while
  327.4 3.1 collective-permute-start
  330.5 51.4 %reduce-scatter.3.cloned.1.call-start = ((), (), s32[]{:S(2)}) async-start(), calls=%async_computation.2 | async-start | bytes 655360 | tf_op jit(solution)/shard_map/while/body/eval_jaxpr/reduce_scatter | solution.py:116
  360.7 37.7 %copy-start.1 = (bf16[64,896]{1,0:T(8,128)(2,1)S(1)}, bf16[64,896]{1,0:T(8,128)(2,1)}, u32[]{:S(2)}) copy-start(bf16[64,896]{1,0:T(8,128)(2,1)} %get-tuple-element.697) | copy-start | bytes 344068 | tf_op jit(solution)/shard_map/while
  361.6 124.6 %all-reduce.9.cloned.1.call-start = ((), (), s32[]{:S(2)}) async-start(), calls=%async_computation.3 | async-start | bytes 2228224 | tf_op jit(solution)/shard_map/while
  487.1 3.1 collective-permute-start
  490.2 51.4 %reduce-scatter.3.cloned.1.call-start = ((), (), s32[]{:S(2)}) async-start(), calls=%async_computation.2 | async-start | bytes 655360 | tf_op jit(solution)/shard_map/while/body/eval_jaxpr/reduce_scatter | solution.py:116
  520.3 37.7 %copy-start.1 = (bf16[64,896]{1,0:T(8,128)(2,1)S(1)}, bf16[64,896]{1,0:T(8,128)(2,1)}, u32[]{:S(2)}) copy-start(bf16[64,896]{1,0:T(8,128)(2,1)} %get-tuple-element.697) | copy-start | bytes 344068 | tf_op jit(solution)/shard_map/while
  521.2 124.6 %all-reduce.9.cloned.1.call-start = ((), (), s32[]{:S(2)}) async-start(), calls=%async_computation.3 | async-start | bytes 2228224 | tf_op jit(solution)/shard_map/while
  646.8 3.1 collective-permute-start
  649.9 51.4 %reduce-scatter.3.cloned.1.call-start = ((), (), s32[]{:S(2)}) async-start(), calls=%async_computation.2 | async-start | bytes 655360 | tf_op jit(solution)/shard_map/while/body/eval_jaxpr/reduce_scatter | solution.py:116
  680.0 37.7 %copy-start.1 = (bf16[64,896]{1,0:T(8,128)(2,1)S(1)}, bf16[64,896]{1,0:T(8,128)(2,1)}, u32[]{:S(2)}) copy-start(bf16[64,896]{1,0:T(8,128)(2,1)} %get-tuple-element.697) | copy-start | bytes 344068 | tf_op jit(solution)/shard_map/while
  680.9 124.6 %all-reduce.9.cloned.1.call-start = ((), (), s32[]{:S(2)}) async-start(), calls=%async_computation.3 | async-start | bytes 2228224 | tf_op jit(solution)/shard_map/while
  806.4 3.1 collective-permute-start
  809.5 177.7 %all-reduce.7.cloned.1.call-start = ((), (), s32[]{:S(2)}) async-start(), calls=%async_computation.1 | async-start | bytes 16777216
  (21 other events, 204.5 us)
Sparse Core Ops, SparseCore 0:
  40.6 21.9 reduce-scatter.2
  80.6 86.2 all-reduce.8
  202.0 20.1 reduce-scatter.2
  240.3 86.2 all-reduce.8
  361.7 20.1 reduce-scatter.2
  399.9 86.2 all-reduce.8
  521.4 20.1 reduce-scatter.2
  559.6 86.2 all-reduce.8
  681.0 20.1 reduce-scatter.2
  719.3 86.2 all-reduce.8
Sparse Core Ops, SparseCore 1:
  818.7 168.4 all-reduce.6
where the time goes:
time: 998 us; the launch traced here: 996 us
  waiting for transfers between devices  695 us (70%)
  blocking collectives  178 us (18%)
  matrix products  57.8 us (6%)
  other arithmetic  22.3 us (2%)
  local copies, waits for them, and re-layouts  16.5 us (2%)
  between operations  16.2 us (2%)
    while x15, waiting for transfers between devices  426 us
    unnamed x2, waiting for transfers between devices  167 us
    all_gather x5, blocking collectives, advance(): gathered_up = lax.all_gather(grad_up, 'dp', axis=0, tiled=True)  117 us
    reduce_scatter x5, waiting for transfers between devices, advance(): lax.psum_scatter(jnp.concatenate([times_t(grad_rows, weight_up), times_t(...  97.6 us
    all_gather x5, blocking collectives, advance(): gathered_low = lax.all_gather(grad_mid, 'mp', axis=0, tiled=True)  61 us
    dot_general x30, matrix products, times_t(): lax.dot_general(left, right, (((1,), (1,)), ((), ())), preferred_element_...  54 us
  transfers between devices with their start and end apart: 16, of which 16 were waited for; matrix products, arithmetic and copies ran while one was open for 1% of the time, Pallas kernels for 0%

commit v1 on v0

--- a/solution.py
+++ b/solution.py
@@ -107,7 +107,9 @@
         first_row = block_safe * rows_block
         top_block = lax.dynamic_slice_in_dim(out_grad, first_row, rows_block, 0)
         grad_up = jnp.where(section_index == section_count - 1, top_block, received)
-        gathered_up = lax.all_gather(grad_up, "dp", axis=0, tiled=True)
+        gathered_up = jnp.concatenate(
+            lax.all_to_all(jnp.stack([grad_up] * lax.axis_size("dp")), "dp", 0, 0), axis=0
+        )
         inputs_up = lax.dynamic_slice_in_dim(acts_upper, first_row, rows_block, 1).reshape(
             dp_count * rows_block, width_hidden
         )

time: 998 us -> 957 us (0.959)
  blocking collectives: 178 us -> 61 us
  waiting for transfers between devices: 695 us -> 740 us
  starting transfers between devices: 6.73 us -> 33 us
    all_gather x5 -> x0, blocking collectives: 117 us -> none  [advance(): gathered_up = lax.all_gather(grad_up, 'dp', axis=0, tiled=True)]
    all_to_all x0 -> x5, waiting for transfers between devices: none -> 50.3 us  [advance(): lax.all_to_all(jnp.stack([grad_up] * lax.axis_size('dp')), 'dp', 0, 0)]
    all_to_all x0 -> x5, starting transfers between devices: none -> 26.1 us  [advance(): lax.all_to_all(jnp.stack([grad_up] * lax.axis_size('dp')), 'dp', 0, 0)]
  transfers between devices with their start and end apart: 16 -> 21, of which waited for: 16 -> 21; matrix products, arithmetic and copies ran while one was open for 1% -> 2% of each run, Pallas kernels for 0% -> 0%
where the time goes in v1:
time: 957 us; the launch traced here: 955 us
  waiting for transfers between devices  740 us (77%)
  blocking collectives  61 us (6%)
  matrix products  58.2 us (6%)
  starting transfers between devices  33 us (3%)
  other arithmetic  22 us (2%)
  local copies, waits for them, and re-layouts  20.5 us (2%)
  between operations  16.2 us (2%)
    while x15, waiting for transfers between devices  426 us
    unnamed x2, waiting for transfers between devices  167 us
    reduce_scatter x5, waiting for transfers between devices, advance(): lax.psum_scatter(jnp.concatenate([times_t(grad_rows, weight_up), times_t(...  92.1 us
    all_gather x5, blocking collectives, advance(): gathered_low = lax.all_gather(grad_mid, 'mp', axis=0, tiled=True)  61 us
    dot_general x30, matrix products, times_t(): lax.dot_general(left, right, (((1,), (1,)), ((), ())), preferred_element_...  54.4 us
    all_to_all x5, waiting for transfers between devices, advance(): lax.all_to_all(jnp.stack([grad_up] * lax.axis_size('dp')), 'dp', 0, 0)  50.3 us
    all_to_all x5, starting transfers between devices, advance(): lax.all_to_all(jnp.stack([grad_up] * lax.axis_size('dp')), 'dp', 0, 0)  26.1 us
  transfers between devices with their start and end apart: 21, of which 21 were waited for; matrix products, arithmetic and copies ran while one was open for 2% of the time, Pallas kernels for 0%

profile of v1, /device:TPU:0, one launch (start us, length us, event | category | flops | bytes accessed | tf_op | source)
XLA Modules:
  0.0 955.1 jit_solution(31331529685006422)
XLA Ops:
  8.1 760.0 %while.21 = (s32[]{:T(128)}, bf16[8,2048]{1,0:T(8,128)(2,1)S(1)}, bf16[32,2048]{1,0:T(8,128)(2,1)S(1)}, f32[4,2,128]{2,1,0:T(2,128)S(1)}, f32[4,2,128]{2,1,0:T(2...) while((s32[]{:T(128)}, bf16[8,2048]{1,0:T(8,128)(2,1)S(1)}, ...), condition=%wide.region_3.4_spmd, body=%wide.region_0.3_spmd.sunk | while | flops 1055576576 | bytes 28222164 | solution.py:179
  9.7 7.1 all-to-all-start
  18.6 9.8 %all-to-all-done = bf16[16,8,2048]{2,1,0:T(8,128)(2,1)S(1)} async-done(((bf16[16,8,2048]{2,1,0:T(8,128)(2,1)}), bf16[16,8,2048]{2,1,0:T(8,128)(2,1)S(1)}, u32[]{:S(2)}, u32[]{:S(2)}) %all-to-all-start) | async-done | bytes 524320 | tf_op jit(solution)/shard_map/while/body/eval_jaxpr/all_to_all | solution.py:111
  35.0 19.1 %reduce-scatter.3.cloned.1.call-done = f32[32,1024]{1,0:T(8,128)} async-done(((f32[128,1024]{1,0:T(8,128)}), f32[32,1024]{1,0:T(8,128)}) %reduce-scatter.3.cloned.1.call-update) | async-done | bytes 131088 | tf_op jit(solution)/shard_map/while/body/eval_jaxpr/reduce_scatter | solution.py:118
  55.1 12.2 %all_gather.10 = bf16[128,896]{1,0:T(8,128)(2,1)S(1)} all-gather(bf16[32,896]{1,0:T(8,128)(2,1)S(1)} %fusion.69), channel_id=1, replica_groups=mesh['section'=2,'dp'=16,'mp'=4] {'mp'}, dimensions={0}, use_global_device_ids=true | all-gather | bytes 286720 | tf_op jit(solution)/shard_map/while/body/eval_jaxpr/all_gather | solution.py:136
  73.4 85.1 %all-reduce.9.cloned.1.call-done = f32[128,2176]{1,0:T(8,128)} async-done(((f32[128,2176]{1,0:T(8,128)}), f32[128,2176]{1,0:T(8,128)}) %all-reduce.9.cloned.1.call-update) | async-done | bytes 1114128 | tf_op jit(solution)/shard_map/while
  164.0 4.8 all-to-all-start
  170.6 10.1 %all-to-all-done = bf16[16,8,2048]{2,1,0:T(8,128)(2,1)S(1)} async-done(((bf16[16,8,2048]{2,1,0:T(8,128)(2,1)}), bf16[16,8,2048]{2,1,0:T(8,128)(2,1)S(1)}, u32[]{:S(2)}, u32[]{:S(2)}) %all-to-all-start) | async-done | bytes 524320 | tf_op jit(solution)/shard_map/while/body/eval_jaxpr/all_to_all | solution.py:111
  187.3 18.3 %reduce-scatter.3.cloned.1.call-done = f32[32,1024]{1,0:T(8,128)} async-done(((f32[128,1024]{1,0:T(8,128)}), f32[32,1024]{1,0:T(8,128)}) %reduce-scatter.3.cloned.1.call-update) | async-done | bytes 131088 | tf_op jit(solution)/shard_map/while/body/eval_jaxpr/reduce_scatter | solution.py:118
  206.5 12.2 %all_gather.10 = bf16[128,896]{1,0:T(8,128)(2,1)S(1)} all-gather(bf16[32,896]{1,0:T(8,128)(2,1)S(1)} %fusion.69), channel_id=1, replica_groups=mesh['section'=2,'dp'=16,'mp'=4] {'mp'}, dimensions={0}, use_global_device_ids=true | all-gather | bytes 286720 | tf_op jit(solution)/shard_map/while/body/eval_jaxpr/all_gather | solution.py:136
  224.8 85.1 %all-reduce.9.cloned.1.call-done = f32[128,2176]{1,0:T(8,128)} async-done(((f32[128,2176]{1,0:T(8,128)}), f32[128,2176]{1,0:T(8,128)}) %all-reduce.9.cloned.1.call-update) | async-done | bytes 1114128 | tf_op jit(solution)/shard_map/while
  322.0 10.1 %all-to-all-done = bf16[16,8,2048]{2,1,0:T(8,128)(2,1)S(1)} async-done(((bf16[16,8,2048]{2,1,0:T(8,128)(2,1)}), bf16[16,8,2048]{2,1,0:T(8,128)(2,1)S(1)}, u32[]{:S(2)}, u32[]{:S(2)}) %all-to-all-start) | async-done | bytes 524320 | tf_op jit(solution)/shard_map/while/body/eval_jaxpr/all_to_all | solution.py:111
  338.7 18.2 %reduce-scatter.3.cloned.1.call-done = f32[32,1024]{1,0:T(8,128)} async-done(((f32[128,1024]{1,0:T(8,128)}), f32[32,1024]{1,0:T(8,128)}) %reduce-scatter.3.cloned.1.call-update) | async-done | bytes 131088 | tf_op jit(solution)/shard_map/while/body/eval_jaxpr/reduce_scatter | solution.py:118
  357.9 12.2 %all_gather.10 = bf16[128,896]{1,0:T(8,128)(2,1)S(1)} all-gather(bf16[32,896]{1,0:T(8,128)(2,1)S(1)} %fusion.69), channel_id=1, replica_groups=mesh['section'=2,'dp'=16,'mp'=4] {'mp'}, dimensions={0}, use_global_device_ids=true | all-gather | bytes 286720 | tf_op jit(solution)/shard_map/while/body/eval_jaxpr/all_gather | solution.py:136
  376.2 85.1 %all-reduce.9.cloned.1.call-done = f32[128,2176]{1,0:T(8,128)} async-done(((f32[128,2176]{1,0:T(8,128)}), f32[128,2176]{1,0:T(8,128)}) %all-reduce.9.cloned.1.call-update) | async-done | bytes 1114128 | tf_op jit(solution)/shard_map/while
  473.4 10.1 %all-to-all-done = bf16[16,8,2048]{2,1,0:T(8,128)(2,1)S(1)} async-done(((bf16[16,8,2048]{2,1,0:T(8,128)(2,1)}), bf16[16,8,2048]{2,1,0:T(8,128)(2,1)S(1)}, u32[]{:S(2)}, u32[]{:S(2)}) %all-to-all-start) | async-done | bytes 524320 | tf_op jit(solution)/shard_map/while/body/eval_jaxpr/all_to_all | solution.py:111
  490.1 18.2 %reduce-scatter.3.cloned.1.call-done = f32[32,1024]{1,0:T(8,128)} async-done(((f32[128,1024]{1,0:T(8,128)}), f32[32,1024]{1,0:T(8,128)}) %reduce-scatter.3.cloned.1.call-update) | async-done | bytes 131088 | tf_op jit(solution)/shard_map/while/body/eval_jaxpr/reduce_scatter | solution.py:118
  509.3 12.2 %all_gather.10 = bf16[128,896]{1,0:T(8,128)(2,1)S(1)} all-gather(bf16[32,896]{1,0:T(8,128)(2,1)S(1)} %fusion.69), channel_id=1, replica_groups=mesh['section'=2,'dp'=16,'mp'=4] {'mp'}, dimensions={0}, use_global_device_ids=true | all-gather | bytes 286720 | tf_op jit(solution)/shard_map/while/body/eval_jaxpr/all_gather | solution.py:136
  527.6 85.1 %all-reduce.9.cloned.1.call-done = f32[128,2176]{1,0:T(8,128)} async-done(((f32[128,2176]{1,0:T(8,128)}), f32[128,2176]{1,0:T(8,128)}) %all-reduce.9.cloned.1.call-update) | async-done | bytes 1114128 | tf_op jit(solution)/shard_map/while
  624.8 10.1 %all-to-all-done = bf16[16,8,2048]{2,1,0:T(8,128)(2,1)S(1)} async-done(((bf16[16,8,2048]{2,1,0:T(8,128)(2,1)}), bf16[16,8,2048]{2,1,0:T(8,128)(2,1)S(1)}, u32[]{:S(2)}, u32[]{:S(2)}) %all-to-all-start) | async-done | bytes 524320 | tf_op jit(solution)/shard_map/while/body/eval_jaxpr/all_to_all | solution.py:111
  641.6 18.2 %reduce-scatter.3.cloned.1.call-done = f32[32,1024]{1,0:T(8,128)} async-done(((f32[128,1024]{1,0:T(8,128)}), f32[32,1024]{1,0:T(8,128)}) %reduce-scatter.3.cloned.1.call-update) | async-done | bytes 131088 | tf_op jit(solution)/shard_map/while/body/eval_jaxpr/reduce_scatter | solution.py:118
  660.7 12.2 %all_gather.10 = bf16[128,896]{1,0:T(8,128)(2,1)S(1)} all-gather(bf16[32,896]{1,0:T(8,128)(2,1)S(1)} %fusion.69), channel_id=1, replica_groups=mesh['section'=2,'dp'=16,'mp'=4] {'mp'}, dimensions={0}, use_global_device_ids=true | all-gather | bytes 286720 | tf_op jit(solution)/shard_map/while/body/eval_jaxpr/all_gather | solution.py:136
  679.0 85.1 %all-reduce.9.cloned.1.call-done = f32[128,2176]{1,0:T(8,128)} async-done(((f32[128,2176]{1,0:T(8,128)}), f32[128,2176]{1,0:T(8,128)}) %all-reduce.9.cloned.1.call-update) | async-done | bytes 1114128 | tf_op jit(solution)/shard_map/while
  779.1 167.0 %all-reduce.7.cloned.1.call-done = f32[2,256,4096]{2,1,0:T(8,128)} async-done(((f32[2,256,4096]{2,1,0:T(8,128)}), f32[2,256,4096]{2,1,0:T(8,128)}) %all-reduce.7.cloned.1.call-update) | async-done | bytes 8388624
  (187 shorter events, 127.2 us)
Async XLA Ops:
  8.1 761.0 %copy-start.3 = (s32[512]{0:T(512)S(1)}, s32[512]{0:T(512)}, u32[]{:S(2)}) copy-start(s32[512]{0:T(512)} %param.26) | copy-start | bytes 6148
  8.1 761.3 %copy-start.4 = (s32[256]{0:T(256)S(1)}, s32[256]{0:T(256)}, u32[]{:S(2)}) copy-start(s32[256]{0:T(256)} %param.27) | copy-start | bytes 3076
  9.7 18.7 %all-to-all-start = ((bf16[16,8,2048]{2,1,0:T(8,128)(2,1)}), bf16[16,8,2048]{2,1,0:T(8,128)(2,1)S(1)}, u32[]{:S(2)}, u32[]{:S(2)}) async-start(bf16[16,8,2048]{2,1,0:T(8,128)(2,1)} %stack.16), calls=%async_computation | async-start | bytes 1048576 | tf_op jit(solution)/shard_map/while/body/eval_jaxpr/all_to_all | solution.py:111
  16.9 37.3 %reduce-scatter.3.cloned.1.call-start = ((), (), s32[]{:S(2)}) async-start(), calls=%async_computation.3 | async-start | bytes 655360 | tf_op jit(solution)/shard_map/while/body/eval_jaxpr/reduce_scatter | solution.py:118
  33.0 37.7 %copy-start = (bf16[64,896]{1,0:T(8,128)(2,1)S(1)}, bf16[64,896]{1,0:T(8,128)(2,1)}, u32[]{:S(2)}) copy-start(bf16[64,896]{1,0:T(8,128)(2,1)} %get-tuple-element.697) | copy-start | bytes 344068 | tf_op jit(solution)/shard_map/while
  33.9 124.6 %all-reduce.9.cloned.1.call-start = ((), (), s32[]{:S(2)}) async-start(), calls=%async_computation.4 | async-start | bytes 2228224 | tf_op jit(solution)/shard_map/while
  159.3 3.1 collective-permute-start
  164.0 16.6 %all-to-all-start = ((bf16[16,8,2048]{2,1,0:T(8,128)(2,1)}), bf16[16,8,2048]{2,1,0:T(8,128)(2,1)S(1)}, u32[]{:S(2)}, u32[]{:S(2)}) async-start(bf16[16,8,2048]{2,1,0:T(8,128)(2,1)} %stack.16), calls=%async_computation | async-start | bytes 1048576 | tf_op jit(solution)/shard_map/while/body/eval_jaxpr/all_to_all | solution.py:111
  168.8 36.8 %reduce-scatter.3.cloned.1.call-start = ((), (), s32[]{:S(2)}) async-start(), calls=%async_computation.3 | async-start | bytes 655360 | tf_op jit(solution)/shard_map/while/body/eval_jaxpr/reduce_scatter | solution.py:118
  186.2 123.7 %all-reduce.9.cloned.1.call-start = ((), (), s32[]{:S(2)}) async-start(), calls=%async_computation.4 | async-start | bytes 2228224 | tf_op jit(solution)/shard_map/while
  310.7 3.1 collective-permute-start
  315.5 16.6 %all-to-all-start = ((bf16[16,8,2048]{2,1,0:T(8,128)(2,1)}), bf16[16,8,2048]{2,1,0:T(8,128)(2,1)S(1)}, u32[]{:S(2)}, u32[]{:S(2)}) async-start(bf16[16,8,2048]{2,1,0:T(8,128)(2,1)} %stack.16), calls=%async_computation | async-start | bytes 1048576 | tf_op jit(solution)/shard_map/while/body/eval_jaxpr/all_to_all | solution.py:111
  320.2 36.7 %reduce-scatter.3.cloned.1.call-start = ((), (), s32[]{:S(2)}) async-start(), calls=%async_computation.3 | async-start | bytes 655360 | tf_op jit(solution)/shard_map/while/body/eval_jaxpr/reduce_scatter | solution.py:118
  337.6 123.7 %all-reduce.9.cloned.1.call-start = ((), (), s32[]{:S(2)}) async-start(), calls=%async_computation.4 | async-start | bytes 2228224 | tf_op jit(solution)/shard_map/while
  462.2 3.1 collective-permute-start
  466.9 16.6 %all-to-all-start = ((bf16[16,8,2048]{2,1,0:T(8,128)(2,1)}), bf16[16,8,2048]{2,1,0:T(8,128)(2,1)S(1)}, u32[]{:S(2)}, u32[]{:S(2)}) async-start(bf16[16,8,2048]{2,1,0:T(8,128)(2,1)} %stack.16), calls=%async_computation | async-start | bytes 1048576 | tf_op jit(solution)/shard_map/while/body/eval_jaxpr/all_to_all | solution.py:111
  471.6 36.7 %reduce-scatter.3.cloned.1.call-start = ((), (), s32[]{:S(2)}) async-start(), calls=%async_computation.3 | async-start | bytes 655360 | tf_op jit(solution)/shard_map/while/body/eval_jaxpr/reduce_scatter | solution.py:118
  489.0 123.7 %all-reduce.9.cloned.1.call-start = ((), (), s32[]{:S(2)}) async-start(), calls=%async_computation.4 | async-start | bytes 2228224 | tf_op jit(solution)/shard_map/while
  613.6 3.1 collective-permute-start
  618.3 16.6 %all-to-all-start = ((bf16[16,8,2048]{2,1,0:T(8,128)(2,1)}), bf16[16,8,2048]{2,1,0:T(8,128)(2,1)S(1)}, u32[]{:S(2)}, u32[]{:S(2)}) async-start(bf16[16,8,2048]{2,1,0:T(8,128)(2,1)} %stack.16), calls=%async_computation | async-start | bytes 1048576 | tf_op jit(solution)/shard_map/while/body/eval_jaxpr/all_to_all | solution.py:111
  623.1 36.7 %reduce-scatter.3.cloned.1.call-start = ((), (), s32[]{:S(2)}) async-start(), calls=%async_computation.3 | async-start | bytes 655360 | tf_op jit(solution)/shard_map/while/body/eval_jaxpr/reduce_scatter | solution.py:118
  640.4 123.7 %all-reduce.9.cloned.1.call-start = ((), (), s32[]{:S(2)}) async-start(), calls=%async_computation.4 | async-start | bytes 2228224 | tf_op jit(solution)/shard_map/while
  765.0 3.1 collective-permute-start
  768.1 177.9 %all-reduce.7.cloned.1.call-start = ((), (), s32[]{:S(2)}) async-start(), calls=%async_computation.2 | async-start | bytes 16777216
  (21 other events, 285.6 us)
Sparse Core Ops, SparseCore 0:
  34.0 20.1 reduce-scatter.2
  72.2 86.1 all-reduce.8
  186.3 19.2 reduce-scatter.2
  223.6 86.2 all-reduce.8
  337.7 19.2 reduce-scatter.2
  375.0 86.2 all-reduce.8
  489.1 19.2 reduce-scatter.2
  526.4 86.2 all-reduce.8
  640.5 19.2 reduce-scatter.2
  677.8 86.2 all-reduce.8
Sparse Core Ops, SparseCore 1:
  777.3 168.7 all-reduce.6
